TPU v7x, 512 devices: a whole 4x8x8 slice. The times are simulated.
512 devices in a mesh: sample: 32 (over y, x), space: 16 (over z, core).
Axes of the slice: x: 4, y: 8, z: 8, core: 2. Of those that a mesh axis runs over, the one named last changes fastest.
Arguments:
- input_field: bfloat16 [32, 64, 64, 4, 128], P('sample', None, 'space'), may hold values from -6 to 6
- out_cotangent: bfloat16 [32, 256, 16, 1, 32], P('sample', None, 'space'), may hold values from -6 to 6
- first_weight: bfloat16 [27, 64, 128], replicated, may hold values from -0.15625 to 0.15625
- second_weight: bfloat16 [27, 128, 256], replicated, may hold values from -0.109375 to 0.109375
Outputs:
- input_grad: bfloat16 [32, 64, 64, 4, 128], P('sample', None, 'space')
- first_grad: bfloat16 [27, 64, 128], replicated
- second_grad: bfloat16 [27, 128, 256], P(None, None, 'space')
All inputs are finite; a program needn't handle non-finite values.
Results may differ from a plain program's by a relative error of at most 0.008.
Values may be sent and summed in bfloat16 or wider, within the bound.
No kernel may reach another device: no remote copies, remote signals or barrier semaphores. Data moves between devices by JAX's collectives and lax.ppermute only.
A program may use at most 64 MiB of HBM per device.

v0:
```python
import math
import jax
import jax.numpy as jnp
from jax import lax
from jax.sharding import PartitionSpec as P


def shifted(value, axis, steps):
    count = lax.axis_size(axis)
    initial, last = (max(0, -steps), min(count, count - steps))
    return lax.ppermute(value, axis, [(source, source + steps) for source in range(initial, last)])


def gradient_silu(values):
    logistic = jax.nn.sigmoid(values)
    return logistic * (1.0 + values * (1.0 - logistic))


def parity_split(padded, extents):
    planes_n, rows_n, cells_n = extents
    channels = padded.shape[0]
    grid = jnp.pad(padded, ((0, 0), (0, 1), (0, 1), (0, 1)))
    grid = grid.reshape(channels, planes_n + 1, 2, rows_n + 1, 2, cells_n + 1, 2)
    return grid.transpose(2, 4, 6, 0, 1, 3, 5)


def tap_block(split, extents, offset):
    planes_n, rows_n, cells_n = extents
    slices = []
    for row_tap in range(3):
        for cell_tap in range(3):
            piece = split[offset % 2, row_tap % 2, cell_tap % 2]
            slices.append(
                piece[
                    :,
                    offset // 2 : offset // 2 + planes_n,
                    row_tap // 2 : row_tap // 2 + rows_n,
                    cell_tap // 2 : cell_tap // 2 + cells_n,
                ]
            )
    stacked = jnp.stack(slices, 0)
    return stacked.reshape(-1, planes_n * rows_n * cells_n)


def make_blocks(padded, extents):
    split = parity_split(padded, extents)
    return [tap_block(split, extents, offset) for offset in range(3)]


def apply_filters(blocks, weight):
    channels = weight.shape[1]
    grouped = weight.reshape(3, 9 * channels, weight.shape[2])
    summed = lax.dot_general(
        grouped[0], blocks[0], (((0,), (0,)), ((), ())), preferred_element_type=jnp.float32
    )
    for offset in (1, 2):
        summed = summed + lax.dot_general(
            grouped[offset],
            blocks[offset],
            (((0,), (0,)), ((), ())),
            preferred_element_type=jnp.float32,
        )
    return summed


def filter_gradient(blocks, deltas):
    products = [
        lax.dot_general(
            tap_rows, deltas, (((1,), (1,)), ((), ())), preferred_element_type=jnp.float32
        )
        for tap_rows in blocks
    ]
    stacked = jnp.stack(products, 0)
    return stacked.reshape(27, -1, deltas.shape[0])


def alternate(taps, spatial):
    leading, central, trailing = (taps[0], taps[1], taps[2])
    planes_in = central.shape[spatial]
    widths = [(0, 0)] * leading.ndim
    upper_pad = list(widths)
    upper_pad[spatial] = (0, 1)
    lower_pad = list(widths)
    lower_pad[spatial] = (1, 0)
    even_part = jnp.pad(leading, upper_pad) + jnp.pad(trailing, lower_pad)
    paired = jnp.stack(
        [lax.slice_in_dim(even_part, 0, planes_in, axis=spatial), central], spatial + 1
    )
    target = list(central.shape)
    target[spatial] = 2 * planes_in
    merged = paired.reshape(target)
    return jnp.concatenate(
        [merged, lax.slice_in_dim(even_part, planes_in, planes_in + 1, axis=spatial)], spatial
    )


def spread_back(weight, deltas, extents):
    channels, filters = (weight.shape[1], weight.shape[2])
    flat_weight = weight.reshape(27 * channels, filters)
    patches = jnp.dot(flat_weight, deltas, preferred_element_type=jnp.float32)
    spread = patches.reshape((3, 3, 3, channels) + tuple(extents))
    spread = alternate(spread, 3)
    spread = alternate(spread, 3)
    spread = alternate(spread, 3)
    return spread


def shards(input_field, out_cotangent, first_weight, second_weight):
    volume = input_field[0]
    chan_in, planes, height, length = volume.shape
    chan_mid = first_weight.shape[2]
    chan_out = second_weight.shape[2]
    groups = lax.axis_size("space")
    samples_n = lax.axis_size("sample")
    first_ext = (planes // 2, height // 2, length // 2)
    second_ext = (planes // 4, height // 4, length // 4)
    lower_rim = shifted(volume[:, planes - 1 :], "space", 1)
    padded = jnp.pad(jnp.concatenate([lower_rim, volume], 1), ((0, 0), (0, 0), (1, 0), (1, 0)))
    first_blocks = make_blocks(padded, first_ext)
    first_pre = apply_filters(first_blocks, first_weight)
    hidden = jax.nn.silu(first_pre).astype(jnp.bfloat16).reshape((chan_mid,) + first_ext)
    cotangent = out_cotangent[0]
    gathered = lax.all_gather(hidden, "space", axis=1, tiled=True)
    gathered_pad = jnp.pad(gathered, ((0, 0), (1, 0), (1, 0), (1, 0)))
    gathered_ext = (gathered.shape[1] // 2, height // 4, length // 4)
    gathered_blocks = make_blocks(gathered_pad, gathered_ext)
    per_group = chan_out // groups
    own_weight = lax.dynamic_slice_in_dim(
        second_weight, lax.axis_index("space") * per_group, per_group, 2
    )
    own_pre = apply_filters(gathered_blocks, own_weight)
    own_cotangent = lax.all_to_all(
        cotangent, "space", split_axis=0, concat_axis=1, tiled=True
    ).reshape(per_group, -1)
    own_delta = (own_cotangent.astype(jnp.float32) * gradient_silu(own_pre)).astype(jnp.bfloat16)
    second_part = filter_gradient(gathered_blocks, own_delta)
    second_delta = lax.all_to_all(
        own_delta.reshape((per_group,) + gathered_ext),
        "space",
        split_axis=1,
        concat_axis=0,
        tiled=True,
    ).reshape(chan_out, -1)
    second_total = lax.psum(second_part, "sample")
    grad_pad = spread_back(second_weight, second_delta, second_ext)
    returned = shifted(grad_pad[:, :1, 1:, 1:], "space", -1)
    interior = grad_pad[:, 1:, 1:, 1:]
    hidden_grad = jnp.concatenate([interior[:, :-1], interior[:, -1:] + returned], 1)
    first_delta = (hidden_grad.reshape(chan_mid, -1) * gradient_silu(first_pre)).astype(
        jnp.bfloat16
    )
    first_part = filter_gradient(first_blocks, first_delta)
    first_total = lax.psum(first_part, ("sample", "space"))
    input_pad = spread_back(first_weight, first_delta, first_ext)
    input_back = shifted(input_pad[:, :1, 1:, 1:].astype(jnp.bfloat16), "space", -1).astype(
        jnp.float32
    )
    input_inner = input_pad[:, 1:, 1:, 1:]
    volume_grad = jnp.concatenate([input_inner[:, :-1], input_inner[:, -1:] + input_back], 1)
    first_scale = 1.0 / math.sqrt(samples_n * groups * first_ext[0] * first_ext[1] * first_ext[2])
    second_scale = 1.0 / math.sqrt(
        samples_n * groups * second_ext[0] * second_ext[1] * second_ext[2]
    )
    input_grad = volume_grad.astype(jnp.bfloat16)[None]
    return (
        input_grad,
        (first_total * first_scale).astype(jnp.bfloat16),
        (second_total * second_scale).astype(jnp.bfloat16),
    )


def solution(mesh):
    placed = (
        P("sample", None, "space", None, None),
        P("sample", None, "space", None, None),
        P(),
        P(),
    )
    return jax.shard_map(
        shards,
        mesh=mesh,
        in_specs=placed,
        out_specs=(P("sample", None, "space", None, None), P(), P(None, None, "space")),
        check_vma=False,
    )
```

profile of v0, /device:TPU:1, one launch (start us, length us, event | category | flops | bytes accessed | tf_op | source)
XLA Modules:
  0.0 558.1 jit_solution(18105045833384356062)
XLA Ops:
  8.1 5.4 collective-permute-start
  13.5 1.8 fusion.69
  15.3 1.7 collective-permute-done
  17.9 1.6 reshape.138
  19.6 2.4 fusion.67
  29.7 1.7 copy.641
  38.6 9.7 %all-to-all-start = ((bf16[16,2,256]{2,1,0:T(2,128)(2,1)}), bf16[16,2,256]{2,1,0:T(2,128)(2,1)S(1)}, u32[]{:S(2)}, u32[]{:S(2)}) async-start(bf16[16,2,256]{2,1,0:T(2,128)(2,1)} %reshape.162), calls=%async_computation | async-start | bytes 32768 | tf_op jit(solution)/shard_map/all_to_all | solution.py:132
  49.4 6.3 %all-to-all-done = bf16[16,2,256]{2,1,0:T(2,128)(2,1)S(1)} async-done(((bf16[16,2,256]{2,1,0:T(2,128)(2,1)}), bf16[16,2,256]{2,1,0:T(2,128)(2,1)S(1)}, u32[]{:S(2)}, u32[]{:S(2)}) %all-to-all-start) | async-done | bytes 16416 | tf_op jit(solution)/shard_map/all_to_all | solution.py:132
  56.0 26.5 %all-gather.2.cloned.1.call-done = bf16[128,32,2,64]{0,3,2,1:T(8,128)(2,1)} async-done(((bf16[128,2,2,64]{0,3,2,1:T(8,128)(2,1)}), bf16[128,32,2,64]{0,3,2,1:T(8,128)(2,1)}) %all-gather.2.cloned.1.call-update) | async-done | bytes 1048592 | tf_op jit(solution)/shard_map/all_gather | solution.py:123
  82.5 2.3 copy.719
  86.2 3.2 fusion.65
  90.6 2.3 fusion.70
  103.1 4.5 all-to-all-start.1
  107.9 7.0 %all-to-all-done.1 = bf16[16,2,256]{2,1,0:T(2,128)(2,1)S(1)} async-done(((bf16[16,2,256]{2,1,0:T(2,128)(2,1)}), bf16[16,2,256]{2,1,0:T(2,128)(2,1)S(1)}, u32[]{:S(2)}, u32[]{:S(2)}) %all-to-all-start.1) | async-done | bytes 16416 | tf_op jit(solution)/shard_map/all_to_all | solution.py:137
  115.0 2.1 convolution_bitcast_fusion
  118.6 2.3 collective-permute-start.1
  122.2 1.9 collective-permute-done.1
  133.5 2.4 copy.673
  135.9 1.4 copy.674
  137.7 1.9 collective-permute-start.2
  140.9 3.5 collective-permute-done.2
  145.5 124.9 %all-reduce.21.cloned.1.call-done = f32[27,128,16]{1,0,2:T(8,128)} async-done(((f32[27,128,16]{1,0,2:T(8,128)}), f32[27,128,16]{1,0,2:T(8,128)}) %all-reduce.21.cloned.1.call-update) | async-done | bytes 221200 | tf_op jit(solution)/shard_map/psum | solution.py:144
  272.1 277.4 %all-reduce.19.cloned.1.call-done = f32[27,64,128]{2,1,0:T(8,128)} async-done(((f32[27,64,128]{2,1,0:T(8,128)}), f32[27,64,128]{2,1,0:T(8,128)}) %all-reduce.19.cloned.1.call-update) | async-done | bytes 884752 | tf_op jit(solution)/shard_map/psum | solution.py:153
  549.5 2.1 multiply_convert_fusion
  (187 shorter events, 47.0 us)
Async XLA Ops:
  7.2 9.9 %copy-start.11 = (bf16[1,64,4,4,128]{4,3,2,1,0:T(4,128)(2,1)S(1)}, bf16[1,64,4,4,128]{4,3,2,1,0:T(4,128)(2,1)}, u32[]{:S(2)}) copy-start(bf16[1,64,4,4,128]{4,3,2,1,0:T(4,128)(2,1)} %param.4) | copy-start | bytes 786436
  7.2 75.3 %all-gather.2.cloned.1.call-start = ((), (), s32[]{:S(2)}) async-start(), calls=%async_computation.2 | async-start | bytes 1114112 | tf_op jit(solution)/shard_map/all_gather | solution.py:123
  8.1 8.9 %collective-permute-start = (bf16[64,1,4,128]{3,2,1,0:T(4,128)(2,1)S(1)}, bf16[64,1,4,128]{3,2,1,0:T(4,128)(2,1)S(1)}, u32[]{:S(2)}, u32[]{:S(2)}) collective-permute-start(bf16[64,1,4,128]{3,2,1,0:T(4,128)(2,1)S(1)} %slice.510), channel_id=1, source_target_pairs={{0,1},{1,2},{2,3},{3,4},{4,5},{5,6},{6,7},{7,8},{8,9},{9,10},{10,1... | collective-permute-start | bytes 196616 | tf_op jit(solution)/shard_map/ppermute | solution.py:11
  31.8 3.2 copy-start.1
  33.9 1.0 copy-start.9
  33.9 1.4 copy-start.10
  34.6 1.1 copy-start.12
  35.0 2.2 copy-start.13
  35.0 13.3 %copy-start = (bf16[27,128,256]{2,1,0:T(8,128)(2,1)S(1)}, bf16[27,128,256]{2,1,0:T(8,128)(2,1)}, u32[]{:S(2)}) copy-start(bf16[27,128,256]{2,1,0:T(8,128)(2,1)} %param.7) | copy-start | bytes 5308420
  38.6 17.0 %all-to-all-start = ((bf16[16,2,256]{2,1,0:T(2,128)(2,1)}), bf16[16,2,256]{2,1,0:T(2,128)(2,1)S(1)}, u32[]{:S(2)}, u32[]{:S(2)}) async-start(bf16[16,2,256]{2,1,0:T(2,128)(2,1)} %reshape.162), calls=%async_computation | async-start | bytes 32768 | tf_op jit(solution)/shard_map/all_to_all | solution.py:132
  99.3 1.0 copy-start.8
  103.1 11.8 %all-to-all-start.1 = ((bf16[16,2,256]{2,1,0:T(2,128)(2,1)}), bf16[16,2,256]{2,1,0:T(2,128)(2,1)S(1)}, u32[]{:S(2)}, u32[]{:S(2)}) async-start(bf16[16,2,256]{2,1,0:T(2,128)(2,1)} %reshape.164), calls=%async_computation.1 | async-start | bytes 32768 | tf_op jit(solution)/shard_map/all_to_all | solution.py:137
  107.5 162.8 %all-reduce.21.cloned.1.call-start = ((), (), s32[]{:S(2)}) async-start(), calls=%async_computation.4 | async-start | bytes 524288 | tf_op jit(solution)/shard_map/psum | solution.py:144
  118.6 5.6 %collective-permute-start.1 = (f32[128,1,2,64]{0,3,2,1:T(8,128)S(1)}, f32[128,1,2,64]{0,3,2,1:T(8,128)S(1)}, u32[]{:S(2)}, u32[]{:S(2)}) collective-permute-start(f32[128,1,2,64]{0,3,2,1:T(8,128)S(1)} %pad_maximum_fusion.15), channel_id=1, source_target_pairs={{1,0},{2,1},{3,2},{4,3},{5,4},{6,5},{7,6},{8,7},{9,8},{10,9},{11,1... | collective-permute-start | bytes 196616 | tf_op jit(solution)/shard_map/ppermute | solution.py:11
  121.9 4.3 copy-start.3
  121.9 427.5 %all-reduce.19.cloned.1.call-start = ((), (), s32[]{:S(2)}) async-start(), calls=%async_computation.3 | async-start | bytes 1769472 | tf_op jit(solution)/shard_map/psum | solution.py:153
  124.3 2.3 copy-start.4
  137.3 2.3 copy-start.2
  137.3 2.3 copy-start.5
  137.5 2.4 copy-start.6
  137.5 2.4 copy-start.7
  137.7 6.7 %collective-permute-start.2 = (bf16[64,1,4,128]{0,3,2,1:T(8,128)(2,1)S(1)}, bf16[64,1,4,128]{0,3,2,1:T(8,128)(2,1)S(1)}, u32[]{:S(2)}, u32[]{:S(2)}) collective-permute-start(bf16[64,1,4,128]{0,3,2,1:T(8,128)(2,1)S(1)} %slice.614), channel_id=1, source_target_pairs={{1,0},{2,1},{3,2},{4,3},{5,4},{6,5},{7,6},{8,7},{9,8},{10,9},{11,1... | collective-permute-start | bytes 196616 | tf_op jit(solution)/shard_map/ppermute | solution.py:11
Sparse Core Ops, SparseCore 0:
  36.7 45.7 all-gather.1
  122.0 148.2 all-reduce.20
  275.4 274.0 all-reduce.18
where the time goes:
time: 559 us; the launch traced here: 558 us
  waiting for transfers between devices  449 us (80%)
  local copies, waits for them, and re-layouts  51.6 us (9%)
  starting transfers between devices  24.1 us (4%)
  between operations  14.8 us (3%)
  other arithmetic  9.86 us (2%)
  matrix products  8.46 us (2%)
    psum x1, waiting for transfers between devices, shards(): first_total = lax.psum(first_part, ('sample', 'space'))  277 us
    psum x1, waiting for transfers between devices, shards(): second_total = lax.psum(second_part, 'sample')  125 us
    all_gather x1, waiting for transfers between devices, shards(): gathered = lax.all_gather(hidden, 'space', axis=1, tiled=True)  26.5 us
    unnamed x80, local copies, waits for them, and re-layouts  13.9 us
  transfers between devices with their start and end apart: 8, of which 8 were waited for; matrix products, arithmetic and copies ran while one was open for 4% of the time, Pallas kernels for 0%

commit v1 on v0

--- a/solution.py
+++ b/solution.py
@@ -141,7 +141,8 @@
         concat_axis=0,
         tiled=True,
     ).reshape(chan_out, -1)
-    second_total = lax.psum(second_part, "sample")
+    pieces = lax.all_gather(second_part, "sample")
+    second_total = jnp.sum(pieces, axis=0)
     grad_pad = spread_back(second_weight, second_delta, second_ext)
     returned = shifted(grad_pad[:, :1, 1:, 1:], "space", -1)
     interior = grad_pad[:, 1:, 1:, 1:]

time: 559 us -> 508 us (0.909)
  waiting for transfers between devices: 449 us -> 370 us
  local copies, waits for them, and re-layouts: 51.6 us -> 66.4 us
  blocking collectives: 0 us -> 11.6 us
  other arithmetic: 9.86 us -> 15.7 us
    psum x1 -> x0, waiting for transfers between devices: 125 us -> none  [shards(): second_total = lax.psum(second_part, 'sample')]
    all_gather x0 -> x1, waiting for transfers between devices: none -> 94.2 us  [shards(): pieces = lax.all_gather(second_part, 'sample')]
    psum x1, waiting for transfers between devices: 277 us -> 234 us  [shards(): first_total = lax.psum(first_part, ('sample', 'space'))]
    all_to_all x0 -> x1, blocking collectives: none -> 11.6 us  [shards(): lax.all_to_all(own_delta.reshape((per_group,) + gathered_ext), 'space', s...]
    all_to_all x1 -> x0, waiting for transfers between devices: 6.96 us -> none  [shards(): lax.all_to_all(own_delta.reshape((per_group,) + gathered_ext), 'space', s...]
    unnamed x80 -> x84, local copies, waits for them, and re-layouts: 13.9 us -> 16.3 us
  transfers between devices with their start and end apart: 8 -> 7, of which waited for: 8 -> 7; matrix products, arithmetic and copies ran while one was open for 4% -> 7% of each run, Pallas kernels for 0% -> 0%
where the time goes in v1:
time: 508 us; the launch traced here: 507 us
  waiting for transfers between devices  370 us (73%)
  local copies, waits for them, and re-layouts  66.4 us (13%)
  starting transfers between devices  19.6 us (4%)
  other arithmetic  15.7 us (3%)
  between operations  14.8 us (3%)
  blocking collectives  11.6 us (2%)
  matrix products  8.62 us (2%)
    psum x1, waiting for transfers between devices, shards(): first_total = lax.psum(first_part, ('sample', 'space'))  234 us
    all_gather x1, waiting for transfers between devices, shards(): pieces = lax.all_gather(second_part, 'sample')  94.2 us
    all_gather x1, waiting for transfers between devices, shards(): gathered = lax.all_gather(hidden, 'space', axis=1, tiled=True)  26.5 us
    unnamed x84, local copies, waits for them, and re-layouts  16.3 us
    all_to_all x1, blocking collectives, shards(): lax.all_to_all(own_delta.reshape((per_group,) + gathered_ext), 'space', s...  11.6 us
  transfers between devices with their start and end apart: 7, of which 7 were waited for; matrix products, arithmetic and copies ran while one was open for 7% of the time, Pallas kernels for 0%

profile of v1, /device:TPU:1, one launch (start us, length us, event | category | flops | bytes accessed | tf_op | source)
XLA Modules:
  0.0 506.7 jit_solution(1931657952110758818)
XLA Ops:
  8.1 5.4 %collective-permute-start = (bf16[64,1,4,128]{3,2,1,0:T(4,128)(2,1)S(1)}, bf16[64,1,4,128]{3,2,1,0:T(4,128)(2,1)S(1)}, u32[]{:S(2)}, u32[]{:S(2)}) collective-permute-start(bf16[64,1,4,128]{3,2,1,0:T(4,128)(2,1)S(1)} %slice.510), channel_id=1, source_target_pairs={{0,1},{1,2},{2,3},{3,4},{4,5},{5,6},{6,7},{7,8},{8,9},{9,10},{10,1... | collective-permute-start | bytes 196616 | tf_op jit(solution)/shard_map/ppermute | solution.py:11
  13.5 1.8 fusion.70
  19.6 2.5 fusion.68
  39.7 9.7 %all-to-all-start = ((bf16[16,2,256]{2,1,0:T(2,128)(2,1)}), bf16[16,2,256]{2,1,0:T(2,128)(2,1)S(1)}, u32[]{:S(2)}, u32[]{:S(2)}) async-start(bf16[16,2,256]{2,1,0:T(2,128)(2,1)} %reshape.158), calls=%async_computation | async-start | bytes 32768 | tf_op jit(solution)/shard_map/all_to_all | solution.py:132
  50.6 6.1 %all-to-all-done = bf16[16,2,256]{2,1,0:T(2,128)(2,1)S(1)} async-done(((bf16[16,2,256]{2,1,0:T(2,128)(2,1)}), bf16[16,2,256]{2,1,0:T(2,128)(2,1)S(1)}, u32[]{:S(2)}, u32[]{:S(2)}) %all-to-all-start) | async-done | bytes 16416 | tf_op jit(solution)/shard_map/all_to_all | solution.py:132
  57.0 26.5 %all-gather.3.cloned.1.call-done = bf16[128,32,2,64]{0,3,2,1:T(8,128)(2,1)} async-done(((bf16[128,2,2,64]{0,3,2,1:T(8,128)(2,1)}), bf16[128,32,2,64]{0,3,2,1:T(8,128)(2,1)}) %all-gather.3.cloned.1.call-update) | async-done | bytes 1048592 | tf_op jit(solution)/shard_map/all_gather | solution.py:123
  83.5 2.3 copy.714
  87.2 3.4 fusion.66
  91.9 1.9 fusion.71
  103.6 11.6 %all_to_all.24 = bf16[16,2,256]{2,1,0:T(2,128)(2,1)S(1)} all-to-all(bf16[16,2,256]{2,1,0:T(2,128)(2,1)S(1)} %reshape.160), channel_id=1, replica_groups=mesh['sample'=32,'space'=16] {'space'}, dimensions={0} | all-to-all | bytes 32768 | tf_op jit(solution)/shard_map/all_to_all | solution.py:137
  115.3 2.1 convolution_bitcast_fusion
  123.0 2.4 collective-permute-start.1
  125.8 2.9 collective-permute-done.1
  131.8 1.9 convolution_bitcast_fusion.2
  139.3 1.8 squeeze.177
  142.7 1.8 stack_squeeze.21
  150.3 3.4 copy.665
  153.6 2.6 pad_add_fusion
  157.9 1.9 collective-permute-start.2
  160.0 4.7 collective-permute-done.2
  165.8 233.8 %all-reduce.18.cloned.1.call-done = f32[27,64,128]{2,1,0:T(8,128)} async-done(((f32[27,64,128]{2,1,0:T(8,128)}), f32[27,64,128]{2,1,0:T(8,128)}) %all-reduce.18.cloned.1.call-update) | async-done | bytes 884752 | tf_op jit(solution)/shard_map/psum | solution.py:154
  399.6 2.1 multiply_convert_fusion
  401.7 94.2 %all-gather.5.cloned.1.call-done = f32[32,27,128,16]{2,3,1,0:T(8,128)} async-done(((f32[1,27,128,16]{2,3,1,0:T(8,128)}), f32[32,27,128,16]{2,3,1,0:T(8,128)}) %all-gather.5.cloned.1.call-update) | async-done | bytes 7077904 | tf_op jit(solution)/shard_map/all_gather | solution.py:144
  495.9 3.5 reduce_sum.9
  (192 shorter events, 61.6 us)
Async XLA Ops:
  7.2 9.9 %copy-start.12 = (bf16[1,64,4,4,128]{4,3,2,1,0:T(4,128)(2,1)S(1)}, bf16[1,64,4,4,128]{4,3,2,1,0:T(4,128)(2,1)}, u32[]{:S(2)}) copy-start(bf16[1,64,4,4,128]{4,3,2,1,0:T(4,128)(2,1)} %param.4) | copy-start | bytes 786436
  7.2 76.4 %all-gather.3.cloned.1.call-start = ((), (), s32[]{:S(2)}) async-start(), calls=%async_computation.2 | async-start | bytes 1114112 | tf_op jit(solution)/shard_map/all_gather | solution.py:123
  8.1 8.9 %collective-permute-start = (bf16[64,1,4,128]{3,2,1,0:T(4,128)(2,1)S(1)}, bf16[64,1,4,128]{3,2,1,0:T(4,128)(2,1)S(1)}, u32[]{:S(2)}, u32[]{:S(2)}) collective-permute-start(bf16[64,1,4,128]{3,2,1,0:T(4,128)(2,1)S(1)} %slice.510), channel_id=1, source_target_pairs={{0,1},{1,2},{2,3},{3,4},{4,5},{5,6},{6,7},{7,8},{8,9},{9,10},{10,1... | collective-permute-start | bytes 196616 | tf_op jit(solution)/shard_map/ppermute | solution.py:11
  22.1 2.9 copy-start.8
  35.0 1.4 copy-start.11
  35.6 1.0 copy-start.13
  36.0 2.2 copy-start.15
  36.0 13.4 %copy-start.4 = (bf16[27,128,256]{2,1,0:T(8,128)(2,1)S(1)}, bf16[27,128,256]{2,1,0:T(8,128)(2,1)}, u32[]{:S(2)}) copy-start(bf16[27,128,256]{2,1,0:T(8,128)(2,1)} %param.7) | copy-start | bytes 5308420
  39.7 17.0 %all-to-all-start = ((bf16[16,2,256]{2,1,0:T(2,128)(2,1)}), bf16[16,2,256]{2,1,0:T(2,128)(2,1)S(1)}, u32[]{:S(2)}, u32[]{:S(2)}) async-start(bf16[16,2,256]{2,1,0:T(2,128)(2,1)} %reshape.158), calls=%async_computation | async-start | bytes 32768 | tf_op jit(solution)/shard_map/all_to_all | solution.py:132
  49.4 350.3 %all-reduce.18.cloned.1.call-start = ((), (), s32[]{:S(2)}) async-start(), calls=%async_computation.3 | async-start | bytes 1769472 | tf_op jit(solution)/shard_map/psum | solution.py:154
  100.0 1.4 copy-start
  100.3 1.2 copy-start.10
  101.3 1.6 copy-start.2
  101.3 1.2 copy-start.9
  123.0 5.8 %copy-start.14 = (f32[128,256]{0,1:T(8,128)S(1)}, f32[128,256]{0,1:T(8,128)}, u32[]{:S(2)}) copy-start(f32[128,256]{0,1:T(8,128)} %get-tuple-element.128) | copy-start | bytes 393220
  123.0 5.7 %collective-permute-start.1 = (f32[128,1,2,64]{0,3,2,1:T(8,128)S(1)}, f32[128,1,2,64]{0,3,2,1:T(8,128)S(1)}, u32[]{:S(2)}, u32[]{:S(2)}) collective-permute-start(f32[128,1,2,64]{0,3,2,1:T(8,128)S(1)} %pad_maximum_fusion.15), channel_id=1, source_target_pairs={{1,0},{2,1},{3,2},{4,3},{5,4},{6,5},{7,6},{8,7},{9,8},{10,9},{11,1... | collective-permute-start | bytes 196616 | tf_op jit(solution)/shard_map/ppermute | solution.py:11
  129.6 1.9 copy-start.1
  130.6 365.3 %all-gather.5.cloned.1.call-start = ((), (), s32[]{:S(2)}) async-start(), calls=%async_computation.4 | async-start | bytes 7299072 | tf_op jit(solution)/shard_map/all_gather | solution.py:144
  133.7 1.1 copy-start.7
  138.3 1.1 copy-start.6
  141.2 1.5 copy-start.5
  147.9 0.9 copy-start.3
  157.9 6.8 %collective-permute-start.2 = (bf16[64,1,4,128]{0,3,2,1:T(8,128)(2,1)S(1)}, bf16[64,1,4,128]{0,3,2,1:T(8,128)(2,1)S(1)}, u32[]{:S(2)}, u32[]{:S(2)}) collective-permute-start(bf16[64,1,4,128]{0,3,2,1:T(8,128)(2,1)S(1)} %slice.614), channel_id=1, source_target_pairs={{1,0},{2,1},{3,2},{4,3},{5,4},{6,5},{7,6},{8,7},{9,8},{10,9},{11,1... | collective-permute-start | bytes 196616 | tf_op jit(solution)/shard_map/ppermute | solution.py:11
Sparse Core Ops, SparseCore 0:
  37.8 45.7 all-gather.2
  130.7 268.8 all-reduce.17
  402.8 93.0 all-gather.4
